TPU v7x, 32 devices: a whole 2x2x4 slice. The times are simulated.
32 devices in a mesh: lat: 8 (over z, y), lon: 4 (over x, core).
Axes of the slice: x: 2, y: 2, z: 4, core: 2. Of those that a mesh axis runs over, the one named last changes fastest.
Arguments:
- grid_fields: bfloat16 [1280, 50, 3, 2560], P('lat', None, None, 'lon'), may hold values from -6 to 6
- legendre: bfloat16 [512, 1280, 640], P(('lat', 'lon')), may hold values from -0.15625 to 0.15625
- wave_of_slot: int32 [512], replicated, may hold values from 0 to 511, as said below
- energy_weight: float32 [3, 640], replicated, may hold values from 0.1 to 10
Outputs:
- spectral: bfloat16 [50, 3, 512, 2, 640], P(None, None, ('lat', 'lon'))
- gram_matrix: float32 [50, 50], replicated
Inputs may be any that keep to these rules, and one draw needn't show every extreme that they name: `wave_of_slot`: every wavenumber 0 to 511 stands in exactly one slot; slot d * 16 + r holds a wavenumber of r * 32 to r * 32 + 31.
All inputs are finite; a program needn't handle non-finite values.
Results may differ from a plain program's by a relative error of at most 0.0043.
Values may be sent and summed in bfloat16 or wider, within the bound.
No kernel may reach another device: no remote copies, remote signals or barrier semaphores. Data moves between devices by JAX's collectives and lax.ppermute only.
A program may use at most 256 MiB of HBM per device.

v0:
```python
import math
import jax
import jax.numpy as jnp
from jax import lax
from jax.sharding import PartitionSpec as P

M = 512
NT = 640
LEV = 3


def make_trig(wave_list, lon_total):
    longitude = jnp.arange(lon_total, dtype=jnp.int32)
    phase_index = longitude[:, None] * wave_list[None, :] % lon_total
    angles = phase_index.astype(jnp.float32) * (2.0 * math.pi / lon_total)
    stacked = jnp.stack([jnp.cos(angles), -jnp.sin(angles)], axis=2)
    return stacked.reshape(lon_total, 2 * wave_list.shape[0]).astype(jnp.bfloat16)


def on_device(grid_fields, legendre, wave_of_slot, energy_weight):
    lat_dev, vectors, levels, lon_dev = grid_fields.shape
    bands = lax.axis_size("lat")
    sectors = lax.axis_size("lon")
    lon_total = lon_dev * sectors
    per_dev = legendre.shape[0]
    degrees = legendre.shape[2]
    fields = vectors * levels
    band_rows = lat_dev // sectors
    norm_scale = 1.0 / math.sqrt(lon_total)
    trig_table = make_trig(wave_of_slot, lon_total)
    moved_rows = lax.all_to_all(grid_fields, "lon", split_axis=0, concat_axis=3, tiled=True)
    product = jnp.dot(
        moved_rows.reshape(-1, lon_total), trig_table, preferred_element_type=jnp.float32
    )
    fourier = product.reshape(band_rows, fields, -1) * norm_scale
    gathered = lax.all_to_all(
        lax.all_to_all(fourier, "lat", split_axis=2, concat_axis=0, tiled=True),
        "lon",
        split_axis=2,
        concat_axis=0,
        tiled=True,
    )
    cols_here = gathered.shape[2]
    columns = gathered.reshape(sectors, bands, band_rows, fields, cols_here).transpose(
        1, 0, 2, 3, 4
    )
    columns = columns.reshape(bands * lat_dev, fields, cols_here)
    columns = columns.reshape(bands * lat_dev, fields, per_dev, 2)
    device_slot = (lax.axis_index("lat") * sectors + lax.axis_index("lon")) * per_dev
    own_waves = lax.dynamic_slice_in_dim(wave_of_slot, device_slot, per_dev, 0)
    degree_index = jnp.arange(degrees, dtype=jnp.int32)
    tri_mask = (degree_index[None, :] >= own_waves[:, None]).astype(jnp.float32)
    legendre_table = legendre.astype(jnp.float32) * tri_mask[:, None, :]
    spectral = jnp.einsum(
        "aftp,tan->ftpn", columns, legendre_table, precision=lax.Precision.HIGHEST
    )
    spectral = spectral.reshape(vectors, levels, per_dev, 2, degrees)
    factor = jnp.where(own_waves == 0, 1.0, 2.0).astype(jnp.float32)
    weighted = spectral * factor[None, None, :, None, None] * energy_weight[None, :, None, None, :]
    partial_value = jnp.dot(
        spectral.reshape(vectors, -1),
        weighted.reshape(vectors, -1).T,
        precision=lax.Precision.HIGHEST,
    )
    gram_matrix = lax.psum(partial_value, ("lat", "lon")) / (LEV * M * NT)
    return (spectral.astype(jnp.bfloat16), gram_matrix)


def solution(mesh):
    placed = (P("lat", None, None, "lon"), P(("lat", "lon"), None, None), P(), P())
    return jax.shard_map(
        on_device,
        mesh=mesh,
        in_specs=placed,
        out_specs=(P(None, None, ("lat", "lon"), None, None), P()),
        check_vma=False,
    )
```

profile of v0, /device:TPU:0, one launch (start us, length us, event | category | flops | bytes accessed | tf_op | source)
XLA Modules:
  0.0 2192.7 jit_solution(3052948345299898282)
XLA Ops:
  0.6 22.1 %copy.47 = bf16[160,50,3,640]{3,1,2,0:T(8,128)(2,1)} copy(bf16[160,50,3,640]{3,0,2,1:T(8,128)(2,1)} %param.4) | data formatting | bytes 61440000 | tf_op args[0]
  22.7 10.0 all-to-all-start
  32.8 22.3 %cosine_convert_fusion = (bf16[2560,512,1]{1,0,2:T(8,128)(2,1)S(1)}, bf16[2560,512,1]{1,0,2:T(8,128)(2,1)S(1)}) fusion(s32[512]{0:T(512)S(1)} %copy-done.1), kind=kLoop, calls=%fused_computation.14 | loop fusion | flops 15728640 | bytes 5244928 | tf_op jit(solution)/shard_map/convert
  55.0 2.8 pad_maximum_fusion
  57.9 13.9 copy.46
  71.8 11.6 convert_element_type.43
  83.4 321.9 %all-to-all-done = bf16[160,50,3,640]{3,1,2,0:T(8,128)(2,1)} async-done(((bf16[160,50,3,640]{3,1,2,0:T(8,128)(2,1)}), bf16[160,50,3,640]{3,1,2,0:T(8,128)(2,1)}, u32[]{:S(2)}, u32[]{:S(2)}) %all-to-all-start) | async-done | bytes 30720032 | tf_op jit(solution)/shard_map/all_to_all | solution.py:31
  405.4 27.3 %copy.48 = bf16[4,40,50,3,640]{4,0,3,2,1:T(4,128)(2,1)} copy(bf16[4,40,50,3,640]{4,2,3,1,0:T(8,128)(2,1)} %bitcast.2) | data formatting | bytes 61440000 | tf_op jit(solution)/shard_map/all_to_all | solution.py:31
  432.6 21.6 copy.67
  454.2 39.4 %multiply_bitcast_fusion = f32[6000,1024]{1,0:T(8,128)} fusion(bf16[2560,1024]{0,1:T(8,128)(2,1)} %convert_element_type.43, bf16[6000,2560]{1,0:T(8,128)(2,1)} %bitcast.48), kind=kOutput, calls=%fused_computation.5 | convolution fusion | flops 31463424000 | bytes 60538880 | tf_op jit(solution)/shard_map/dot_general | solution.py:32
  493.6 19.6 mul.105
  513.3 43.6 %copy.49 = f32[40,150,1024]{1,0,2:T(8,128)} copy(f32[40,150,1024]{2,1,0:T(8,128)} %mul.105) | data formatting | bytes 49152000 | tf_op jit(solution)/shard_map/mul | solution.py:35
  556.9 915.7 %all_to_all.48 = f32[40,150,1024]{1,0,2:T(8,128)} all-to-all(f32[40,150,1024]{1,0,2:T(8,128)} %copy.49), channel_id=1, replica_groups=mesh['lat'=8,'lon'=4] {'lat'}, dimensions={2} | all-to-all | bytes 49152000 | tf_op jit(solution)/shard_map/all_to_all | solution.py:37
  1472.6 36.6 %copy.51 = f32[8,40,150,128]{3,1,0,2:T(8,128)} copy(f32[8,40,150,128]{2,1,3,0:T(8,128)} %bitcast.44) | data formatting | bytes 49152000 | tf_op jit(solution)/shard_map/all_to_all | solution.py:37
  1509.2 28.0 %copy.52 = f32[320,150,128]{0,1,2:T(8,128)} copy(f32[320,150,128]{2,0,1:T(8,128)} %bitcast.47) | data formatting | bytes 49152000 | tf_op jit(solution)/shard_map/all_to_all | solution.py:37
  1537.2 9.6 all-to-all-start.2
  1546.9 0.2 mul.109
  1547.1 0.8 compare_select_fusion
  1548.0 322.3 %all-to-all-done.2 = f32[320,150,128]{0,1,2:T(8,128)} async-done(((f32[320,150,128]{0,1,2:T(8,128)}), f32[320,150,128]{0,1,2:T(8,128)}, u32[]{:S(2)}, u32[]{:S(2)}) %all-to-all-start.2) | async-done | bytes 24576032 | tf_op jit(solution)/shard_map/all_to_all | solution.py:36
  1870.3 46.2 %copy.54 = f32[4,320,150,32]{2,3,1,0:T(8,128)} copy(f32[4,320,150,32]{1,2,3,0:T(8,128)} %bitcast.11) | data formatting | bytes 49152000 | tf_op jit(solution)/shard_map/all_to_all | solution.py:36
  1916.5 39.3 %copy.55 = f32[8,4,40,150,32]{3,2,1,0,4:T(8,128)} copy(f32[8,4,40,150,32]{3,4,2,0,1:T(8,128)} %bitcast.45) | data formatting | bytes 49152000 | tf_op jit(solution)/shard_map/transpose | solution.py:44
  1955.7 76.5 %fusion = f32[16,640,150,2]{1,2,3,0:T(8,128)} fusion(f32[1280,150,16,2]{1,0,3,2:T(8,128)} %bitcast.43, bf16[16,1280,640]{2,1,0:T(8,128)(2,1)} %param.5, f32[16,640]{1,0:T(8,128)S(1)} %fusion.11), kind=kOutput, calls=%fused_computation | convolution fusion | flops 47212134400 | bytes 63119360 | tf_op jit(solution)/shard_map/aftp,tan->ftpn/dot_general | solution.py:54
  2032.2 8.0 copy.70
  2040.3 11.4 copy.60
  2051.6 22.5 %copy.58 = f32[150,16,2,640]{3,2,1,0:T(2,128)} copy(f32[150,16,2,640]{3,0,2,1:T(8,128)} %bitcast.42) | data formatting | bytes 24576000 | tf_op jit(solution)/shard_map/aftp,tan->ftpn/transpose | solution.py:54
  2074.1 15.4 reshape_reshape.7
  2089.5 13.2 fusion.5
  2102.6 18.4 copy.59
  2121.0 15.1 mul.112
  2136.1 16.4 fusion.12
  2152.5 39.1 %psum.7 = f32[50,50]{1,0:T(8,128)S(1)} all-reduce(f32[50,50]{1,0:T(8,128)S(1)} %fusion.12), channel_id=1, replica_groups=mesh['lat'=8,'lon'=4] {'lat','lon'}, use_global_device_ids=true, to_apply=%region_0.1 | all-reduce | flops 2500 | bytes 20000 | tf_op jit(solution)/shard_map/psum | solution.py:65
  2191.6 0.6 broadcast_multiply_fusion
  (6 shorter events, 0.1 us)
Async XLA Ops:
  22.7 10.0 copy-start.1
  22.7 382.6 %all-to-all-start = ((bf16[160,50,3,640]{3,1,2,0:T(8,128)(2,1)}), bf16[160,50,3,640]{3,1,2,0:T(8,128)(2,1)}, u32[]{:S(2)}, u32[]{:S(2)}) async-start(bf16[160,50,3,640]{3,1,2,0:T(8,128)(2,1)} %copy.47), calls=%async_computation | async-start | bytes 68812800 | tf_op jit(solution)/shard_map/all_to_all | solution.py:31
  1537.2 9.7 copy-start
  1537.2 333.1 %all-to-all-start.2 = ((f32[320,150,128]{0,1,2:T(8,128)}), f32[320,150,128]{0,1,2:T(8,128)}, u32[]{:S(2)}, u32[]{:S(2)}) async-start(f32[320,150,128]{0,1,2:T(8,128)} %copy.52), calls=%async_computation.2 | async-start | bytes 59768832 | tf_op jit(solution)/shard_map/all_to_all | solution.py:36
where the time goes:
time: 2210 us; the launch traced here: 2190 us
  blocking collectives  955 us (43%)
  waiting for transfers between devices  644 us (29%)
  local copies, waits for them, and re-layouts  401 us (18%)
  matrix products  132 us (6%)
  other arithmetic  39.7 us (2%)
    all_to_all x1, blocking collectives, on_device(): lax.all_to_all(fourier, 'lat', split_axis=2, concat_axis=0, tiled=True)  916 us
    all_to_all x1, waiting for transfers between devices, on_device(): lax.all_to_all(lax.all_to_all(fourier, 'lat', split_axis=2, concat_axis=0...  322 us
    all_to_all x1, waiting for transfers between devices, on_device(): lax.all_to_all(grid_fields, 'lon', split_axis=0, concat_axis=3, tiled=True)  322 us
    dot_general x1, matrix products, on_device(): jnp.einsum('aftp,tan->ftpn', columns, legendre_table, precision=lax.Preci...  76.5 us
    all_to_all x2, local copies, waits for them, and re-layouts, on_device(): lax.all_to_all(fourier, 'lat', split_axis=2, concat_axis=0, tiled=True)  64.6 us
    mul x2, local copies, waits for them, and re-layouts, on_device(): fourier = product.reshape(band_rows, fields, -1) * norm_scale  63.2 us
    unnamed x7, local copies, waits for them, and re-layouts  55 us
    all_to_all x1, local copies, waits for them, and re-layouts, on_device(): lax.all_to_all(lax.all_to_all(fourier, 'lat', split_axis=2, concat_axis=0...  46.2 us
  transfers between devices with their start and end apart: 2, of which 2 were waited for; matrix products, arithmetic and copies ran while one was open for 2% of the time, Pallas kernels for 0%

commit v1 on v0

--- a/solution.py
+++ b/solution.py
@@ -1,3 +1,4 @@
+import functools
 import math
 import jax
 import jax.numpy as jnp
@@ -7,6 +8,18 @@
 M = 512
 NT = 640
 LEV = 3
+
+
+def _note_core(buf, named_axis):
+    return jnp.concatenate(
+        lax.all_to_all(
+            jnp.stack(jnp.split(buf, lax.psum(1, named_axis), 2), axis=0), named_axis, 0, 0
+        ),
+        0,
+    )
+
+
+points_note = functools.partial(_note_core, named_axis="lon")
 
 
 def make_trig(wave_list, lon_total):
@@ -33,13 +46,7 @@
         moved_rows.reshape(-1, lon_total), trig_table, preferred_element_type=jnp.float32
     )
     fourier = product.reshape(band_rows, fields, -1) * norm_scale
-    gathered = lax.all_to_all(
-        lax.all_to_all(fourier, "lat", split_axis=2, concat_axis=0, tiled=True),
-        "lon",
-        split_axis=2,
-        concat_axis=0,
-        tiled=True,
-    )
+    gathered = points_note(lax.all_to_all(fourier, "lat", split_axis=2, concat_axis=0, tiled=True))
     cols_here = gathered.shape[2]
     columns = gathered.reshape(sectors, bands, band_rows, fields, cols_here).transpose(
         1, 0, 2, 3, 4

time: 2210 us -> 2330 us (1.054)
  local copies, waits for them, and re-layouts: 401 us -> 506 us
    another operation x0 -> x5, local copies, waits for them, and re-layouts: none -> 132 us  [_note_core(): jnp.stack(jnp.split(buf, lax.psum(1, named_axis), 2), axis=0)]
    all_to_all x2 -> x1, local copies, waits for them, and re-layouts: 64.6 us -> 36.6 us  [on_device(): lax.all_to_all(fourier, 'lat', split_axis=2, concat_axis=0, tiled=True)]
where the time goes in v1:
time: 2330 us; the launch traced here: 2310 us
  blocking collectives  955 us (41%)
  waiting for transfers between devices  640 us (27%)
  local copies, waits for them, and re-layouts  506 us (22%)
  matrix products  133 us (6%)
  other arithmetic  60.3 us (3%)
    all_to_all x1, blocking collectives, on_device(): lax.all_to_all(fourier, 'lat', split_axis=2, concat_axis=0, tiled=True)  916 us
    all_to_all x1, waiting for transfers between devices, on_device(): lax.all_to_all(grid_fields, 'lon', split_axis=0, concat_axis=3, tiled=True)  322 us
    all_to_all x1, waiting for transfers between devices, _note_core(): lax.all_to_all(jnp.stack(jnp.split(buf, lax.psum(1, named_axis), 2), axis...  318 us
    another operation x5, local copies, waits for them, and re-layouts, _note_core(): jnp.stack(jnp.split(buf, lax.psum(1, named_axis), 2), axis=0)  132 us
    dot_general x1, matrix products, on_device(): jnp.einsum('aftp,tan->ftpn', columns, legendre_table, precision=lax.Preci...  76.9 us
    mul x2, local copies, waits for them, and re-layouts, on_device(): fourier = product.reshape(band_rows, fields, -1) * norm_scale  63.2 us
    unnamed x7, local copies, waits for them, and re-layouts  53.7 us
  transfers between devices with their start and end apart: 2, of which 2 were waited for; matrix products, arithmetic and copies ran while one was open for 2% of the time, Pallas kernels for 0%

profile of v1, /device:TPU:0, one launch (start us, length us, event | category | flops | bytes accessed | tf_op | source)
XLA Modules:
  0.0 2313.7 jit_solution(3045876017830567920)
XLA Ops:
  0.6 22.1 copy.50
  22.7 10.0 all-to-all-start
  32.7 22.3 cosine_convert_fusion
  57.8 13.9 copy.49
  71.7 11.6 convert_element_type.43
  83.3 322.0 %all-to-all-done = bf16[160,50,3,640]{3,1,2,0:T(8,128)(2,1)} async-done(((bf16[160,50,3,640]{3,1,2,0:T(8,128)(2,1)}), bf16[160,50,3,640]{3,1,2,0:T(8,128)(2,1)}, u32[]{:S(2)}, u32[]{:S(2)}) %all-to-all-start) | async-done | bytes 30720032 | tf_op jit(solution)/shard_map/all_to_all | solution.py:44
  405.3 27.3 %copy.51 = bf16[4,40,50,3,640]{4,0,3,2,1:T(4,128)(2,1)} copy(bf16[4,40,50,3,640]{4,2,3,1,0:T(8,128)(2,1)} %bitcast.2) | data formatting | bytes 61440000 | tf_op jit(solution)/shard_map/all_to_all | solution.py:44
  432.6 21.6 copy.71
  454.1 39.4 %multiply_bitcast_fusion = f32[6000,1024]{1,0:T(8,128)} fusion(bf16[2560,1024]{0,1:T(8,128)(2,1)} %convert_element_type.43, bf16[6000,2560]{1,0:T(8,128)(2,1)} %bitcast.53), kind=kOutput, calls=%fused_computation.10 | convolution fusion | flops 31463424000 | bytes 60538880 | tf_op jit(solution)/shard_map/dot_general | solution.py:45
  493.5 19.6 mul.105
  513.2 43.5 %copy.52 = f32[40,150,1024]{1,0,2:T(8,128)} copy(f32[40,150,1024]{2,1,0:T(8,128)} %mul.105) | data formatting | bytes 49152000 | tf_op jit(solution)/shard_map/mul | solution.py:48
  556.7 915.9 %all_to_all.38 = f32[40,150,1024]{1,0,2:T(8,128)} all-to-all(f32[40,150,1024]{1,0,2:T(8,128)} %copy.52), channel_id=1, replica_groups=mesh['lat'=8,'lon'=4] {'lat'}, dimensions={2} | all-to-all | bytes 49152000 | tf_op jit(solution)/shard_map/all_to_all | solution.py:49
  1472.6 36.6 %copy.54 = f32[8,40,150,128]{3,1,0,2:T(8,128)} copy(f32[8,40,150,128]{2,1,3,0:T(8,128)} %bitcast.50) | data formatting | bytes 49152000 | tf_op jit(solution)/shard_map/all_to_all | solution.py:49
  1509.2 62.8 %slice_bitcast_fusion.3 = (f32[1,320,150,32]{3,1,2,0:T(8,128)}, f32[1,320,150,32]{3,1,2,0:T(8,128)}, f32[1,320,150,32]{3,1,2,0:T(8,128)}, f32[1,320,150,32]{3,1,2,0:T(8,128)}) fusion(f32[320,150,128]{2,0,1:T(8,128)} %bitcast.47), kind=kLoop, calls=%fused_computation.9 | loop fusion | bytes 49152000 | tf_op jit(solution)/shard_map/stack | solution.py:16
  1572.0 17.2 copy.55
  1589.2 17.2 copy.56
  1606.4 17.2 copy.57
  1623.6 17.2 copy.58
  1640.8 20.7 pad_maximum_fusion
  1671.9 318.1 %all-to-all-done.2 = f32[4,320,150,32]{1,3,2,0:T(8,128)} async-done(((f32[4,320,150,32]{1,3,2,0:T(8,128)}), f32[4,320,150,32]{1,3,2,0:T(8,128)}, u32[]{:S(2)}, u32[]{:S(2)}) %all-to-all-start.2) | async-done | bytes 24576032 | tf_op jit(solution)/shard_map/all_to_all | solution.py:15
  1990.0 46.4 %copy.59 = f32[4,320,150,32]{2,3,1,0:T(8,128)} copy(f32[4,320,150,32]{1,3,2,0:T(8,128)} %all-to-all-done.2) | data formatting | bytes 49152000 | tf_op jit(solution)/shard_map/all_to_all | solution.py:15
  2036.4 39.1 %copy.60 = f32[8,4,40,150,32]{3,2,1,0,4:T(8,128)} copy(f32[8,4,40,150,32]{3,4,2,0,1:T(8,128)} %bitcast.51) | data formatting | bytes 49152000 | tf_op jit(solution)/shard_map/transpose | solution.py:51
  2075.5 76.9 %fusion = f32[16,640,150,2]{1,2,3,0:T(8,128)} fusion(f32[1280,150,16,2]{1,0,3,2:T(8,128)} %bitcast.49, bf16[16,1280,640]{2,1,0:T(8,128)(2,1)} %param.5, f32[16,640]{1,0:T(8,128)S(1)} %fusion.11), kind=kOutput, calls=%fused_computation | convolution fusion | flops 47212134400 | bytes 63119360 | tf_op jit(solution)/shard_map/aftp,tan->ftpn/dot_general | solution.py:61
  2152.4 10.6 copy.74
  2163.0 13.1 fusion.5
  2176.1 18.4 copy.64
  2194.5 15.2 mul.112
  2209.7 22.6 copy.63
  2232.3 15.1 reshape_reshape.11
  2247.4 16.2 fusion.12
  2263.6 39.1 %psum.7 = f32[50,50]{1,0:T(8,128)S(1)} all-reduce(f32[50,50]{1,0:T(8,128)S(1)} %fusion.12), channel_id=1, replica_groups=mesh['lat'=8,'lon'=4] {'lat','lon'}, use_global_device_ids=true, to_apply=%region_0.1 | all-reduce | flops 2500 | bytes 20000 | tf_op jit(solution)/shard_map/psum | solution.py:72
  2303.4 10.1 copy.65
  (11 shorter events, 13.8 us)
Async XLA Ops:
  22.7 10.0 copy-start.1
  22.7 382.6 %all-to-all-start = ((bf16[160,50,3,640]{3,1,2,0:T(8,128)(2,1)}), bf16[160,50,3,640]{3,1,2,0:T(8,128)(2,1)}, u32[]{:S(2)}, u32[]{:S(2)}) async-start(bf16[160,50,3,640]{3,1,2,0:T(8,128)(2,1)} %copy.50), calls=%async_computation | async-start | bytes 68812800 | tf_op jit(solution)/shard_map/all_to_all | solution.py:44
  1661.5 9.2 copy-start
  1661.5 328.5 %all-to-all-start.2 = ((f32[4,320,150,32]{1,3,2,0:T(8,128)}), f32[4,320,150,32]{1,3,2,0:T(8,128)}, u32[]{:S(2)}, u32[]{:S(2)}) async-start(f32[4,320,150,32]{1,3,2,0:T(8,128)} %pad_maximum_fusion), calls=%async_computation.2 | async-start | bytes 58982400 | tf_op jit(solution)/shard_map/all_to_all | solution.py:15
